TPU v7x, 32 devices: a whole 2x2x4 slice. The times are simulated.
32 devices in a mesh: band: 16 (over z, y, x), member: 2 (over core).
Axes of the slice: x: 2, y: 2, z: 4, core: 2. Of those that a mesh axis runs over, the one named last changes fastest.
Arguments:
- scaled_atmosphere_field: float32 [80, 4096], P(None, 'band'), may hold values from -6 to 6
- perturbation: bfloat16 [2, 80, 4096], P('member', None, 'band'), may hold values from -6 to 6
- target: bfloat16 [2, 80, 4096], P('member', None, 'band'), may hold values from -6 to 6
- weight_map: bfloat16 [80, 4096], P(None, 'band'), may hold values from 0.01 to 10
- enc_send: int32 [16, 16, 32], P('band'), may hold values from -1 to 255, as said below
- enc_recv: int32 [16, 16, 32], P('band'), may hold values from -1 to 255, as said below
- dec_send: int32 [16, 16, 32], P('band'), may hold values from -1 to 255, as said below
- dec_recv: int32 [16, 16, 32], P('band'), may hold values from -1 to 255, as said below
- lattice_lift_matrix: bfloat16 [80, 512], replicated, may hold values from -0.625 to 0.625
- mixing_rescale_factor: float32 [512], replicated, may hold values from 0.1 to 1.9
- expand_matrix: bfloat16 [512, 512], replicated, may hold values from -0.25 to 0.25
- contract_matrix: bfloat16 [512, 512], replicated, may hold values from -0.25 to 0.25
- readout_matrix: bfloat16 [512, 80], replicated, may hold values from -0.25 to 0.25
Outputs:
- student_outputs: float32 [2, 80, 4096], P('member', None, 'band')
- mesh_grad: bfloat16 [2, 4096, 512], P('member', 'band')
- grad_up: float32 [2, 512, 512], P('member')
- grad_down: float32 [2, 512, 512], P('member')
- grad_dec: float32 [2, 512, 80], P('member')
- grad_gain: float32 [2, 512], P('member')
Inputs may be any that keep to these rules, and one draw needn't show every extreme that they name: enc_send[s, d, k] is a local grid cell of band s (0 to 255) or -1 for an empty slot; in every draw one band fills all its slots and one partition receives full blocks of 32 from every band. enc_recv[d, s, k] is a local mesh node of partition d, and -1 exactly where enc_send[s, d, k] is -1. dec_send[s, d, k] is a local mesh node of partition s or -1 for an empty slot; in every draw one partition fills all its slots and one band receives full blocks of 32 from every partition. dec_recv[d, s, k] is a local grid cell of band d, and -1 exactly where dec_send[s, d, k] is -1.
All inputs are finite; a program needn't handle non-finite values.
Results may differ from a plain program's by a relative error of at most 0.0062.
Values may be sent and summed in bfloat16 or wider, within the bound.
No kernel may reach another device: no remote copies, remote signals or barrier semaphores. Data moves between devices by JAX's collectives and lax.ppermute only.
A program may use at most 64 MiB of HBM per device.

v0:
```python
import math
import jax
import jax.numpy as jnp
from jax import lax
from jax.sharding import PartitionSpec as P

MESH_DEV = 256
smooth_sq = 0.01
norm_eps = 1e-05


def slope(diff):
    return diff * lax.rsqrt(diff * diff + smooth_sq)


def embed_columns(columns, lattice_lift_matrix):
    pre_act = lax.dot_general(
        columns, lattice_lift_matrix, (((0,), (0,)), ((), ())), preferred_element_type=jnp.float32
    )
    return jax.nn.silu(pre_act).astype(jnp.bfloat16)


def body(
    scaled_atmosphere_field,
    perturbation,
    target,
    weight_map,
    enc_send,
    enc_recv,
    dec_send,
    dec_recv,
    lattice_lift_matrix,
    mixing_rescale_factor,
    expand_matrix,
    contract_matrix,
    readout_matrix,
):
    highest = lax.Precision.HIGHEST
    band_count = lax.axis_size("band")
    channels, grid_rows = scaled_atmosphere_field.shape
    width = lattice_lift_matrix.shape[1]
    node_rows = MESH_DEV
    enc_width = enc_send.shape[2]
    dec_width = dec_send.shape[2]
    cell_ids = jnp.arange(grid_rows, dtype=jnp.int32)
    node_ids = jnp.arange(node_rows, dtype=jnp.int32)
    inputs_b = (scaled_atmosphere_field + perturbation[0].astype(jnp.float32)).astype(jnp.bfloat16)
    send_index = enc_send[0].reshape(-1)
    picker = (send_index[:, None] == cell_ids[None, :]).astype(jnp.bfloat16)
    latent = embed_columns(inputs_b, lattice_lift_matrix)
    outgoing = jnp.dot(picker, latent, preferred_element_type=jnp.float32).astype(jnp.bfloat16)
    arrived = lax.all_to_all(
        outgoing.reshape(band_count, enc_width, width),
        "band",
        split_axis=0,
        concat_axis=0,
        tiled=True,
    )
    slot_rows = arrived.reshape(-1, width)
    recv_index = enc_recv[0].reshape(-1)
    landing = (node_ids[:, None] == recv_index[None, :]).astype(jnp.bfloat16)
    summed = jnp.dot(landing, slot_rows, preferred_element_type=jnp.float32)
    edge_count = jnp.sum(landing.astype(jnp.float32), axis=1, keepdims=True)
    mesh_state = summed / jnp.maximum(edge_count, 1.0)
    recip = lax.rsqrt(jnp.mean(mesh_state * mesh_state, axis=1, keepdims=True) + norm_eps)
    normed_b = (mesh_state * recip * mixing_rescale_factor).astype(jnp.bfloat16)
    hidden_pre = jnp.dot(normed_b, expand_matrix, preferred_element_type=jnp.float32)
    hidden_b = jax.nn.silu(hidden_pre).astype(jnp.bfloat16)
    mesh_next = mesh_state + jnp.dot(hidden_b, contract_matrix, preferred_element_type=jnp.float32)
    next_b = mesh_next.astype(jnp.bfloat16)
    dec_index = dec_send[0].reshape(-1)
    mesh_picker = (dec_index[:, None] == node_ids[None, :]).astype(jnp.bfloat16)
    cell_index = dec_recv[0].reshape(-1)
    fill_map = (cell_ids[:, None] == cell_index[None, :]).astype(jnp.bfloat16)
    grid_count = jnp.sum(fill_map.astype(jnp.float32), axis=1)
    inverse = 1.0 / jnp.maximum(grid_count, 1.0)
    projected = lax.dot_general(
        readout_matrix, next_b, (((0,), (1,)), ((), ())), preferred_element_type=jnp.float32
    ).astype(jnp.bfloat16)
    chosen = lax.dot_general(
        projected, mesh_picker, (((1,), (1,)), ((), ())), preferred_element_type=jnp.float32
    ).astype(jnp.bfloat16)
    slot_values = lax.all_to_all(
        chosen.reshape(channels, band_count, dec_width),
        "band",
        split_axis=1,
        concat_axis=1,
        tiled=True,
    ).reshape(channels, -1)
    grid_sum = lax.dot_general(
        slot_values, fill_map, (((1,), (1,)), ((), ())), preferred_element_type=jnp.float32
    )
    student_outputs = scaled_atmosphere_field + grid_sum * inverse[None, :]
    all_pred, all_target = (
        lax.all_gather(student_outputs[None], "member", axis=0, tiled=True),
        lax.all_gather(target.astype(jnp.float32), "member", axis=0, tiled=True),
    )
    teacher_terms = jnp.sum(slope(student_outputs[None] - all_target), axis=0)
    own_terms = jnp.sum(slope(student_outputs[None] - all_pred), axis=0)
    pred_grad = weight_map.astype(jnp.float32) * (teacher_terms - own_terms)
    scaled = pred_grad * inverse[None, :]
    slot_grad = jnp.dot(scaled, fill_map.astype(jnp.float32), precision=highest)
    dec_f32 = readout_matrix.astype(jnp.float32)
    picker_f32 = mesh_picker.astype(jnp.float32)
    returned = lax.all_to_all(
        slot_grad.reshape(channels, band_count, dec_width),
        "band",
        split_axis=1,
        concat_axis=1,
        tiled=True,
    ).reshape(channels, -1)
    node_grad = jnp.dot(returned, picker_f32, precision=highest)
    next_grad = lax.dot_general(node_grad, dec_f32, (((0,), (1,)), ((), ())), precision=highest)
    dec_part = lax.dot_general(
        next_b.astype(jnp.float32), node_grad, (((0,), (1,)), ((), ())), precision=highest
    )
    down_part = lax.dot_general(
        hidden_b.astype(jnp.float32), next_grad, (((0,), (0,)), ((), ())), precision=highest
    )
    hidden_grad = lax.dot_general(
        next_grad, contract_matrix.astype(jnp.float32), (((1,), (1,)), ((), ())), precision=highest
    )
    sigma = jax.nn.sigmoid(hidden_pre)
    pre_grad = hidden_grad * sigma * (1.0 + hidden_pre * (1.0 - sigma))
    up_part = lax.dot_general(
        normed_b.astype(jnp.float32), pre_grad, (((0,), (0,)), ((), ())), precision=highest
    )
    normed_grad = lax.dot_general(
        pre_grad, expand_matrix.astype(jnp.float32), (((1,), (1,)), ((), ())), precision=highest
    )
    gain_part = jnp.sum(normed_grad * mesh_state * recip, axis=0)
    gained = normed_grad * mixing_rescale_factor
    state_grad = (
        next_grad
        + recip * gained
        - mesh_state
        * (recip * recip * recip)
        * jnp.mean(gained * mesh_state, axis=1, keepdims=True)
    )
    up_sum, down_sum, dec_sum, gain_sum = lax.psum(
        (up_part, down_part, dec_part, gain_part), "band"
    )
    factor = 1.0 / math.sqrt(band_count * node_rows)
    return (
        student_outputs[None],
        state_grad.astype(jnp.bfloat16)[None],
        (up_sum * factor)[None],
        (down_sum * factor)[None],
        (dec_sum * factor)[None],
        (gain_sum * factor)[None],
    )


def solution(mesh):
    return jax.shard_map(
        body,
        mesh=mesh,
        in_specs=(
            P(None, "band"),
            P("member", None, "band"),
            P("member", None, "band"),
            P(None, "band"),
            P("band", None, None),
            P("band", None, None),
            P("band", None, None),
            P("band", None, None),
            P(),
            P(),
            P(),
            P(),
            P(),
        ),
        out_specs=(
            P("member", None, "band"),
            P("member", "band", None),
            P("member", None, None),
            P("member", None, None),
            P("member", None, None),
            P("member", None),
        ),
        check_vma=False,
    )
```

profile of v0, /device:TPU:0, one launch (start us, length us, event | category | flops | bytes accessed | tf_op | source)
XLA Modules:
  0.0 213.1 jit_solution(13352040407852293177)
XLA Ops:
  7.2 0.8 eq.64
  8.0 2.4 %convolution_convert_fusion = bf16[512,512]{1,0:T(8,128)(2,1)} fusion(bf16[80,512]{1,0:T(8,128)(2,1)} %param.21, s32[512]{0:T(512)S(1)} %eq.64, f32[80,256]{1,0:T(8,128)} %param.13, bf16[1,80,256]{2,1,0:T(8,128)(2,1)} %param.14), kind=kOutput, calls=%fused_computation | convolution fusion | flops 156299264 | bytes 731136 | tf_op jit(solution)/shard_map/dot_general | solution.py:51
  10.4 8.5 %all-to-all-start = ((bf16[16,32,512]{2,1,0:T(8,128)(2,1)}), bf16[16,32,512]{2,1,0:T(8,128)(2,1)S(1)}, u32[]{:S(2)}, u32[]{:S(2)}) async-start(bf16[16,32,512]{2,1,0:T(8,128)(2,1)} %bitcast.1), calls=%async_computation | async-start | bytes 1048576 | tf_op jit(solution)/shard_map/all_to_all | solution.py:52
  19.0 0.6 copy-done.7
  19.7 1.9 all_gather.6
  21.9 12.0 %all-to-all-done = bf16[16,32,512]{2,1,0:T(8,128)(2,1)S(1)} async-done(((bf16[16,32,512]{2,1,0:T(8,128)(2,1)}), bf16[16,32,512]{2,1,0:T(8,128)(2,1)S(1)}, u32[]{:S(2)}, u32[]{:S(2)}) %all-to-all-start) | async-done | bytes 524320 | tf_op jit(solution)/shard_map/all_to_all | solution.py:52
  33.9 0.4 multiply_reduce_fusion.2
  34.4 0.7 copy-done.5
  35.4 0.7 copy-done.9
  36.1 0.3 fusion.1
  36.4 0.5 copy-done.2
  37.0 0.5 convolution_convert_fusion.1
  37.4 0.8 copy.23
  38.2 4.1 %all-to-all-start.1 = ((bf16[80,16,32]{0,2,1:T(8,128)(2,1)}), bf16[80,16,32]{0,2,1:T(8,128)(2,1)S(1)}, u32[]{:S(2)}, u32[]{:S(2)}) async-start(bf16[80,16,32]{0,2,1:T(8,128)(2,1)} %bitcast.3), calls=%async_computation.1 | async-start | bytes 262144 | tf_op jit(solution)/shard_map/all_to_all | solution.py:83
  42.3 7.7 %all-to-all-done.1 = bf16[80,16,32]{0,2,1:T(8,128)(2,1)S(1)} async-done(((bf16[80,16,32]{0,2,1:T(8,128)(2,1)}), bf16[80,16,32]{0,2,1:T(8,128)(2,1)S(1)}, u32[]{:S(2)}, u32[]{:S(2)}) %all-to-all-start.1) | async-done | bytes 81952 | tf_op jit(solution)/shard_map/all_to_all | solution.py:83
  50.3 1.9 all-gather
  52.3 0.7 copy-done.3
  53.0 0.6 fusion.3
  53.6 13.0 %all_to_all.15 = f32[80,16,32]{0,2,1:T(8,128)S(1)} all-to-all(f32[80,16,32]{0,2,1:T(8,128)S(1)} %bitcast.42), channel_id=1, replica_groups=mesh['band'=16,'member'=2] {'band'}, dimensions={1} | all-to-all | bytes 327680 | tf_op jit(solution)/shard_map/all_to_all | solution.py:105
  66.7 0.5 fusion.5
  67.2 0.9 fusion.30
  68.1 0.4 fusion.29
  68.5 0.7 fusion
  69.2 1.7 fusion.28
  70.9 1.7 fusion.26
  72.7 0.7 multiply_reduce_fusion
  73.4 40.0 %psum.31 = f32[512]{0:T(512)S(1)} all-reduce(f32[512]{0:T(512)S(1)} %get-tuple-element.6), channel_id=1, replica_groups=mesh['band'=16,'member'=2] {'band'}, use_global_device_ids=true, to_apply=%region_10.11 | all-reduce | flops 512 | bytes 4096 | tf_op jit(solution)/shard_map/psum | solution.py:140
  113.4 0.6 broadcast_multiply_fusion
  114.0 0.9 fusion.7
  114.8 86.7 %all-reduce.3.cloned.1.call-done = (f32[512,512]{1,0:T(8,128)}, f32[512,512]{1,0:T(8,128)}, f32[512,80]{0,1:T(8,128)}) async-done(((f32[512,512]{1,0:T(8,128)}, f32[512,512]{1,0:T(8,128)}, f32[512,80]{0,1:T(8,128)}), (f32[512,512]{1,0:T(8,128)}, f32[512,512]{1,0:T(8,128)}, f32[512,80]{0,1:T(8,128)})) %all-reduce.3.cloned.1.call-update) | async-done | bytes 2261008 | tf_op jit(solution)/shard_map/psum | solution.py:140
  201.6 1.6 multiply_bitcast_fusion.2
  203.2 3.1 %multiply_bitcast_fusion = (f32[1,512,512]{2,1,0:T(8,128)}, f32[1,512,512]{2,1,0:T(8,128)}) fusion(f32[512,512]{1,0:T(8,128)} %get-tuple-element.11, f32[512,512]{1,0:T(8,128)} %get-tuple-element.10), kind=kLoop, calls=%fused_computation.10 | loop fusion | flops 524288 | bytes 4194304 | tf_op jit(solution)/shard_map/broadcast_in_dim | solution.py:148
  (32 shorter events, 1.3 us)
Async XLA Ops:
  7.2 27.2 %copy-start = (bf16[512,512]{1,0:T(8,128)(2,1)S(1)}, bf16[512,512]{1,0:T(8,128)(2,1)}, u32[]{:S(2)}) copy-start(bf16[512,512]{1,0:T(8,128)(2,1)} %param.23) | copy-start | bytes 1572868
  10.4 8.5 %copy-start.6 = (s32[1,16,32]{2,1,0:T(8,128)S(1)}, s32[1,16,32]{2,1,0:T(8,128)}, u32[]{:S(2)}) copy-start(s32[1,16,32]{2,1,0:T(8,128)} %param.20) | copy-start | bytes 6148
  10.4 9.3 %copy-start.4 = (bf16[1,80,256]{2,1,0:T(8,128)(2,1)S(1)}, bf16[1,80,256]{2,1,0:T(8,128)(2,1)}, u32[]{:S(2)}) copy-start(bf16[1,80,256]{2,1,0:T(8,128)(2,1)} %param.15) | copy-start | bytes 122884
  10.4 23.6 %all-to-all-start = ((bf16[16,32,512]{2,1,0:T(8,128)(2,1)}), bf16[16,32,512]{2,1,0:T(8,128)(2,1)S(1)}, u32[]{:S(2)}, u32[]{:S(2)}) async-start(bf16[16,32,512]{2,1,0:T(8,128)(2,1)} %bitcast.1), calls=%async_computation | async-start | bytes 1048576 | tf_op jit(solution)/shard_map/all_to_all | solution.py:52
  18.9 0.7 copy-start.7
  18.9 0.8 copy-start.8
  34.3 0.7 copy-start.5
  35.0 1.0 copy-start.9
  36.1 0.9 copy-start.2
  38.2 11.9 %copy-start.10 = (f32[80,256]{1,0:T(8,128)S(1)}, f32[80,256]{1,0:T(8,128)}, u32[]{:S(2)}) copy-start(f32[80,256]{1,0:T(8,128)} %param.13) | copy-start | bytes 245764
  38.2 11.9 %all-to-all-start.1 = ((bf16[80,16,32]{0,2,1:T(8,128)(2,1)}), bf16[80,16,32]{0,2,1:T(8,128)(2,1)S(1)}, u32[]{:S(2)}, u32[]{:S(2)}) async-start(bf16[80,16,32]{0,2,1:T(8,128)(2,1)} %bitcast.3), calls=%async_computation.1 | async-start | bytes 262144 | tf_op jit(solution)/shard_map/all_to_all | solution.py:83
  42.3 159.3 %all-reduce.3.cloned.1.call-start = ((), (), s32[]{:S(2)}) async-start(), calls=%async_computation.3 | async-start | bytes 4521984 | tf_op jit(solution)/shard_map/psum | solution.py:140
  50.3 1.9 copy-start.1
  52.2 0.8 copy-start.3
Sparse Core Ops, SparseCore 0:
  72.8 128.7 all-reduce.2
where the time goes:
time: 214 us; the launch traced here: 213 us
  waiting for transfers between devices  106 us (50%)
  blocking collectives  56.9 us (27%)
  between operations  14.2 us (7%)
  starting transfers between devices  12.6 us (6%)
  matrix products  11.4 us (5%)
  other arithmetic  6.51 us (3%)
  local copies, waits for them, and re-layouts  5.08 us (2%)
    psum x1, waiting for transfers between devices, body(): lax.psum((up_part, down_part, dec_part, gain_part), 'band')  86.7 us
    psum x1, blocking collectives, body(): lax.psum((up_part, down_part, dec_part, gain_part), 'band')  40 us
    all_to_all x1, blocking collectives, body(): lax.all_to_all(slot_grad.reshape(channels, band_count, dec_width), 'band'...  13 us
    all_to_all x1, waiting for transfers between devices, body(): lax.all_to_all(outgoing.reshape(band_count, enc_width, width), 'band', sp...  12 us
    all_to_all x1, starting transfers between devices, body(): lax.all_to_all(outgoing.reshape(band_count, enc_width, width), 'band', sp...  8.47 us
    all_to_all x1, waiting for transfers between devices, body(): lax.all_to_all(chosen.reshape(channels, band_count, dec_width), 'band', s...  7.73 us
  transfers between devices with their start and end apart: 3, of which 3 were waited for; matrix products, arithmetic and copies ran while one was open for 1% of the time, Pallas kernels for 0%

commit v1 on v0

--- a/solution.py
+++ b/solution.py
@@ -35,6 +35,18 @@
     contract_matrix,
     readout_matrix,
 ):
+
+    def search_leaves_in(x_in, chip_axis="band"):
+        return jnp.concatenate(
+            lax.all_to_all(
+                jnp.stack(jnp.split(x_in, lax.axis_size(chip_axis), axis=1)),
+                axis_name=chip_axis,
+                split_axis=0,
+                concat_axis=0,
+            ),
+            axis=1,
+        )
+
     highest = lax.Precision.HIGHEST
     band_count = lax.axis_size("band")
     channels, grid_rows = scaled_atmosphere_field.shape
@@ -80,13 +92,9 @@
     chosen = lax.dot_general(
         projected, mesh_picker, (((1,), (1,)), ((), ())), preferred_element_type=jnp.float32
     ).astype(jnp.bfloat16)
-    slot_values = lax.all_to_all(
-        chosen.reshape(channels, band_count, dec_width),
-        "band",
-        split_axis=1,
-        concat_axis=1,
-        tiled=True,
-    ).reshape(channels, -1)
+    slot_values = search_leaves_in(chosen.reshape(channels, band_count, dec_width)).reshape(
+        channels, -1
+    )
     grid_sum = lax.dot_general(
         slot_values, fill_map, (((1,), (1,)), ((), ())), preferred_element_type=jnp.float32
     )

time: 214 us -> 223 us (1.042)
  local copies, waits for them, and re-layouts: 5.08 us -> 14 us
    unnamed x22 -> x37, local copies, waits for them, and re-layouts: 3.26 us -> 12.2 us
where the time goes in v1:
time: 223 us; the launch traced here: 222 us
  waiting for transfers between devices  107 us (48%)
  blocking collectives  56.9 us (26%)
  between operations  14.2 us (6%)
  local copies, waits for them, and re-layouts  14 us (6%)
  starting transfers between devices  12.6 us (6%)
  matrix products  11.4 us (5%)
  other arithmetic  6.51 us (3%)
    psum x1, waiting for transfers between devices, body(): lax.psum((up_part, down_part, dec_part, gain_part), 'band')  86.8 us
    psum x1, blocking collectives, body(): lax.psum((up_part, down_part, dec_part, gain_part), 'band')  40 us
    all_to_all x1, blocking collectives, body(): lax.all_to_all(slot_grad.reshape(channels, band_count, dec_width), 'band'...  13 us
    unnamed x37, local copies, waits for them, and re-layouts  12.2 us
    all_to_all x1, waiting for transfers between devices, body(): lax.all_to_all(outgoing.reshape(band_count, enc_width, width), 'band', sp...  12 us
    all_to_all x1, starting transfers between devices, body(): lax.all_to_all(outgoing.reshape(band_count, enc_width, width), 'band', sp...  8.47 us
    all_to_all x1, waiting for transfers between devices, search_leaves_in(): lax.all_to_all(jnp.stack(jnp.split(x_in, lax.axis_size(chip_axis), axis=1...  7.73 us
  transfers between devices with their start and end apart: 3, of which 3 were waited for; matrix products, arithmetic and copies ran while one was open for 1% of the time, Pallas kernels for 0%

profile of v1, /device:TPU:0, one launch (start us, length us, event | category | flops | bytes accessed | tf_op | source)
XLA Modules:
  0.0 222.1 jit_solution(12960877795679446161)
XLA Ops:
  7.2 0.8 eq.64
  8.0 2.4 %convolution_convert_fusion = bf16[512,512]{1,0:T(8,128)(2,1)} fusion(bf16[80,512]{1,0:T(8,128)(2,1)} %param.21, s32[512]{0:T(512)S(1)} %eq.64, f32[80,256]{1,0:T(8,128)} %param.13, bf16[1,80,256]{2,1,0:T(8,128)(2,1)} %param.14), kind=kOutput, calls=%fused_computation | convolution fusion | flops 156299264 | bytes 731136 | tf_op jit(solution)/shard_map/dot_general | solution.py:63
  10.4 8.5 %all-to-all-start = ((bf16[16,32,512]{2,1,0:T(8,128)(2,1)}), bf16[16,32,512]{2,1,0:T(8,128)(2,1)S(1)}, u32[]{:S(2)}, u32[]{:S(2)}) async-start(bf16[16,32,512]{2,1,0:T(8,128)(2,1)} %bitcast.1), calls=%async_computation | async-start | bytes 1048576 | tf_op jit(solution)/shard_map/all_to_all | solution.py:64
  19.7 1.9 all_gather.6
  21.9 12.0 %all-to-all-done = bf16[16,32,512]{2,1,0:T(8,128)(2,1)S(1)} async-done(((bf16[16,32,512]{2,1,0:T(8,128)(2,1)}), bf16[16,32,512]{2,1,0:T(8,128)(2,1)S(1)}, u32[]{:S(2)}, u32[]{:S(2)}) %all-to-all-start) | async-done | bytes 524320 | tf_op jit(solution)/shard_map/all_to_all | solution.py:64
  34.4 0.7 copy-done.5
  35.4 0.7 copy-done.9
  37.5 0.6 constant_dynamic-update-slice_fusion.15
  38.2 0.6 constant_dynamic-update-slice_fusion.14
  38.8 0.6 constant_dynamic-update-slice_fusion.13
  39.4 0.6 constant_dynamic-update-slice_fusion.12
  40.6 0.6 constant_dynamic-update-slice_fusion.10
  41.1 0.6 constant_dynamic-update-slice_fusion.9
  42.9 0.6 constant_dynamic-update-slice_fusion.6
  44.7 0.6 constant_dynamic-update-slice_fusion.3
  46.5 0.6 constant_dynamic-update-slice_fusion
  47.1 4.1 %all-to-all-start.1 = ((bf16[16,80,1,32]{1,3,2,0:T(8,128)(2,1)}), bf16[16,80,1,32]{1,3,2,0:T(8,128)(2,1)S(1)}, u32[]{:S(2)}, u32[]{:S(2)}) async-start(bf16[16,80,1,32]{1,3,2,0:T(8,128)(2,1)} %constant_dynamic-update-slice_fusion), calls=%async_computation.1 | async-start | bytes 262144 | tf_op jit(solution)/shard_map/all_to_all | solution.py:41
  51.3 7.7 %all-to-all-done.1 = bf16[16,80,1,32]{1,3,2,0:T(8,128)(2,1)S(1)} async-done(((bf16[16,80,1,32]{1,3,2,0:T(8,128)(2,1)}), bf16[16,80,1,32]{1,3,2,0:T(8,128)(2,1)S(1)}, u32[]{:S(2)}, u32[]{:S(2)}) %all-to-all-start.1) | async-done | bytes 81952 | tf_op jit(solution)/shard_map/all_to_all | solution.py:41
  59.3 1.9 all-gather
  61.3 0.7 copy-done.3
  62.0 0.6 fusion.3
  62.6 13.0 %all_to_all.15 = f32[80,16,32]{0,2,1:T(8,128)S(1)} all-to-all(f32[80,16,32]{0,2,1:T(8,128)S(1)} %bitcast.108), channel_id=1, replica_groups=mesh['band'=16,'member'=2] {'band'}, dimensions={1} | all-to-all | bytes 327680 | tf_op jit(solution)/shard_map/all_to_all | solution.py:113
  76.1 0.9 fusion.30
  77.5 0.7 fusion
  78.2 1.7 fusion.28
  79.9 1.7 fusion.26
  81.6 0.7 multiply_reduce_fusion
  82.4 40.0 %psum.31 = f32[512]{0:T(512)S(1)} all-reduce(f32[512]{0:T(512)S(1)} %get-tuple-element.6), channel_id=1, replica_groups=mesh['band'=16,'member'=2] {'band'}, use_global_device_ids=true, to_apply=%region_10.11 | all-reduce | flops 512 | bytes 4096 | tf_op jit(solution)/shard_map/psum | solution.py:148
  122.9 0.9 fusion.7
  123.8 86.8 %all-reduce.3.cloned.1.call-done = (f32[512,512]{1,0:T(8,128)}, f32[512,512]{1,0:T(8,128)}, f32[512,80]{0,1:T(8,128)}) async-done(((f32[512,512]{1,0:T(8,128)}, f32[512,512]{1,0:T(8,128)}, f32[512,80]{0,1:T(8,128)}), (f32[512,512]{1,0:T(8,128)}, f32[512,512]{1,0:T(8,128)}, f32[512,80]{0,1:T(8,128)})) %all-reduce.3.cloned.1.call-update) | async-done | bytes 2261008 | tf_op jit(solution)/shard_map/psum | solution.py:148
  210.6 1.6 multiply_bitcast_fusion.2
  212.2 3.1 %multiply_bitcast_fusion = (f32[1,512,512]{2,1,0:T(8,128)}, f32[1,512,512]{2,1,0:T(8,128)}) fusion(f32[512,512]{1,0:T(8,128)} %get-tuple-element.11, f32[512,512]{1,0:T(8,128)} %get-tuple-element.10), kind=kLoop, calls=%fused_computation.10 | loop fusion | flops 524288 | bytes 4194304 | tf_op jit(solution)/shard_map/broadcast_in_dim | solution.py:156
  (48 shorter events, 9.4 us)
Async XLA Ops:
  7.2 27.2 %copy-start = (bf16[512,512]{1,0:T(8,128)(2,1)S(1)}, bf16[512,512]{1,0:T(8,128)(2,1)}, u32[]{:S(2)}) copy-start(bf16[512,512]{1,0:T(8,128)(2,1)} %param.23) | copy-start | bytes 1572868
  10.4 8.5 %copy-start.6 = (s32[1,16,32]{2,1,0:T(8,128)S(1)}, s32[1,16,32]{2,1,0:T(8,128)}, u32[]{:S(2)}) copy-start(s32[1,16,32]{2,1,0:T(8,128)} %param.20) | copy-start | bytes 6148
  10.4 9.3 %copy-start.4 = (bf16[1,80,256]{2,1,0:T(8,128)(2,1)S(1)}, bf16[1,80,256]{2,1,0:T(8,128)(2,1)}, u32[]{:S(2)}) copy-start(bf16[1,80,256]{2,1,0:T(8,128)(2,1)} %param.15) | copy-start | bytes 122884
  10.4 23.6 %all-to-all-start = ((bf16[16,32,512]{2,1,0:T(8,128)(2,1)}), bf16[16,32,512]{2,1,0:T(8,128)(2,1)S(1)}, u32[]{:S(2)}, u32[]{:S(2)}) async-start(bf16[16,32,512]{2,1,0:T(8,128)(2,1)} %bitcast.1), calls=%async_computation | async-start | bytes 1048576 | tf_op jit(solution)/shard_map/all_to_all | solution.py:64
  18.9 0.7 copy-start.7
  18.9 0.8 copy-start.8
  34.3 0.7 copy-start.5
  35.0 1.0 copy-start.9
  36.1 0.9 copy-start.2
  47.1 11.9 %copy-start.10 = (f32[80,256]{1,0:T(8,128)S(1)}, f32[80,256]{1,0:T(8,128)}, u32[]{:S(2)}) copy-start(f32[80,256]{1,0:T(8,128)} %param.13) | copy-start | bytes 245764
  47.1 11.9 %all-to-all-start.1 = ((bf16[16,80,1,32]{1,3,2,0:T(8,128)(2,1)}), bf16[16,80,1,32]{1,3,2,0:T(8,128)(2,1)S(1)}, u32[]{:S(2)}, u32[]{:S(2)}) async-start(bf16[16,80,1,32]{1,3,2,0:T(8,128)(2,1)} %constant_dynamic-update-slice_fusion), calls=%async_computation.1 | async-start | bytes 262144 | tf_op jit(solution)/shard_map/all_to_all | solution.py:41
  51.2 159.4 %all-reduce.3.cloned.1.call-start = ((), (), s32[]{:S(2)}) async-start(), calls=%async_computation.3 | async-start | bytes 4521984 | tf_op jit(solution)/shard_map/psum | solution.py:148
  59.3 1.9 copy-start.1
  61.2 0.8 copy-start.3
Sparse Core Ops, SparseCore 0:
  81.7 128.8 all-reduce.2
